TPU v7x, 256 devices: a whole 4x4x8 slice. The times are simulated.
256 devices in a mesh: dp: 16 (over z, y_lo), dep: 4 (over x), hgt: 4 (over y_hi, core).
Axes of the slice: x: 4, y: 4 (y_hi: 2, y_lo: 2; y = y_hi * 2 + y_lo), z: 8, core: 2. Of those that a mesh axis runs over, the one named last changes fastest.
Arguments:
- volume: bfloat16 [16, 32, 8, 32, 128], P('dp', None, 'dep', 'hgt'), may hold values from -6 to 6
- kernel_first: bfloat16 [27, 64, 32], replicated, may hold values from -0.21875 to 0.21875
- kernel_second: bfloat16 [27, 128, 64], replicated, may hold values from -0.15625 to 0.15625
- cotangent: bfloat16 [16, 128, 8, 32, 128], P('dp', None, 'dep', 'hgt'), may hold values from -0.01171875 to 0.01171875
Outputs:
- features: bfloat16 [16, 128, 8, 32, 128], P('dp', None, 'dep', 'hgt')
- grad_first: float32 [27, 64, 32], P(None, 'dp')
- grad_second: float32 [27, 128, 64], P(None, 'dp')
All inputs are finite; a program needn't handle non-finite values.
Results may differ from a plain program's by a relative error of at most 0.0049.
Values may be sent and summed in bfloat16 or wider, within the bound.
A program may use at most 64 MiB of HBM per device.

v0:
```python
import jax
import jax.numpy as jnp
from jax import lax
from jax.sharding import PartitionSpec as P

OFFSETS = [
    (first, second, third) for first in (-1, 0, 1) for second in (-1, 0, 1) for third in (-1, 0, 1)
]


def extended_2(x, sides, width):
    for axis, dim in sides:
        size, length = (lax.axis_size(axis), x.shape[dim])
        up = [(i, (i + 1) % size) for i in range(size - 1)]
        down = [(j, i) for i, j in up]
        last = lax.slice_in_dim(x, length - width, length, axis=dim)
        leading = lax.slice_in_dim(x, 0, width, axis=dim)
        before = lax.ppermute(last, axis, up)
        after = lax.ppermute(leading, axis, down)
        x = jnp.concatenate([before, x, after], axis=dim)
    return x


def widen(field):
    return jnp.pad(field, ((0, 0), (0, 0), (0, 0), (0, 0), (1, 1)))


def window(padded, shift_d, shift_h, shift_w, depth, height, width):
    return padded[
        :,
        :,
        1 + shift_d : 1 + shift_d + depth,
        1 + shift_h : 1 + shift_h + height,
        1 + shift_w : 1 + shift_w + width,
    ]


def convolve(extended, kernel, depth, height, width):
    padded = widen(extended)
    total = None
    for number, shift in enumerate(OFFSETS):
        piece = window(padded, shift[0], shift[1], shift[2], depth, height, width)
        term = jnp.einsum(
            "oi,bidhw->bodhw", kernel[number], piece, preferred_element_type=jnp.float32
        )
        total = term if total is None else total + term
    return total


def kernel_grad(upstream, extended, depth, height, width):
    padded = widen(extended)
    parts = []
    for shift in OFFSETS:
        piece = window(padded, shift[0], shift[1], shift[2], depth, height, width)
        parts.append(
            jnp.einsum("bodhw,bidhw->oi", upstream, piece, preferred_element_type=jnp.float32)
        )
    return jnp.stack(parts)


def per_device(volume, kernel_first, kernel_second, cotangent):
    depth, height, width = (volume.shape[2], volume.shape[3], volume.shape[4])
    vol_rim = extended_2(volume, (("dep", 2), ("hgt", 3)), 1)
    pre = convolve(vol_rim, kernel_first, depth, height, width)
    hidden = jax.nn.silu(pre).astype(jnp.bfloat16)
    hidden_rim = extended_2(hidden, (("dep", 2), ("hgt", 3)), 1)
    features = convolve(hidden_rim, kernel_second, depth, height, width).astype(jnp.bfloat16)
    cot_rim = extended_2(cotangent, (("dep", 2), ("hgt", 3)), 1)
    grad_second = kernel_grad(cotangent, hidden_rim, depth, height, width)
    padded_cot = widen(cot_rim)
    back = None
    for number, shift in enumerate(OFFSETS):
        piece = window(padded_cot, -shift[0], -shift[1], -shift[2], depth, height, width)
        term = jnp.einsum(
            "oi,bodhw->bidhw", kernel_second[number], piece, preferred_element_type=jnp.float32
        )
        back = term if back is None else back + term
    sigma = jax.nn.sigmoid(pre)
    delta = (back * (sigma * (1.0 + pre * (1.0 - sigma)))).astype(jnp.bfloat16)
    grad_first = kernel_grad(delta, vol_rim, depth, height, width)
    summed = lax.psum((grad_first, grad_second), ("dep", "hgt"))
    grad_first, grad_second = (
        lax.psum_scatter(summed[0], "dp", scatter_dimension=1, tiled=True),
        lax.psum_scatter(summed[1], "dp", scatter_dimension=1, tiled=True),
    )
    return (features, grad_first, grad_second)


def solution(mesh):
    placed = (P("dp", None, "dep", "hgt", None), P(), P(), P("dp", None, "dep", "hgt", None))
    return jax.shard_map(
        per_device,
        mesh=mesh,
        in_specs=placed,
        out_specs=(P("dp", None, "dep", "hgt", None), P(None, "dp", None), P(None, "dp", None)),
        check_vma=False,
    )
```

profile of v0, /device:TPU:8, one launch (start us, length us, event | category | flops | bytes accessed | tf_op | source)
XLA Modules:
  0.0 418.0 jit_solution(17139515704096667886)
XLA Ops:
  7.2 0.9 copy.50
  8.2 3.5 collective-permute-start
  11.7 1.4 collective-permute-start.1
  13.2 1.2 copy.56
  14.4 4.6 %collective-permute-start.8 = (bf16[1,128,1,8,128]{4,1,3,2,0:T(8,128)(2,1)S(1)}, bf16[1,128,1,8,128]{4,1,3,2,0:T(8,128)(2,1)S(1)}, u32[]{:S(2)}, u32[]{:S(2)}) collective-permute-start(bf16[1,128,1,8,128]{4,1,3,2,0:T(8,128)(2,1)S(1)} %get-tuple-element.14), channel_id=1, source_target_pairs={{0,4},{4,8},{8,12},{1,5},{5,9},{9,13},{2,6},{6,10},{10,14},{3,7},{... | collective-permute-start | bytes 786440 | tf_op jit(solution)/shard_map/ppermute | solution.py:18
  19.0 1.3 collective-permute-start.9
  20.4 1.3 collective-permute-start.2
  21.7 1.3 collective-permute-start.3
  23.3 4.0 collective-permute-done.3
  35.5 4.6 %collective-permute-start.4 = (bf16[1,64,1,8,128]{4,1,3,2,0:T(8,128)(2,1)S(1)}, bf16[1,64,1,8,128]{4,1,3,2,0:T(8,128)(2,1)S(1)}, u32[]{:S(2)}, u32[]{:S(2)}) collective-permute-start(bf16[1,64,1,8,128]{4,1,3,2,0:T(8,128)(2,1)S(1)} %get-tuple-element.19), channel_id=1, source_target_pairs={{0,4},{4,8},{8,12},{1,5},{5,9},{9,13},{2,6},{6,10},{10,14},{3,7},{... | collective-permute-start | bytes 393224 | tf_op jit(solution)/shard_map/ppermute | solution.py:18
  40.1 1.3 collective-permute-start.5
  41.6 0.9 collective-permute-done.4
  42.6 4.4 %collective-permute-done.5 = bf16[1,64,1,8,128]{4,1,3,2,0:T(8,128)(2,1)S(1)} collective-permute-done((bf16[1,64,1,8,128]{4,1,3,2,0:T(8,128)(2,1)S(1)}, bf16[1,64,1,8,128]{4,1,3,2,0:T(8,128)(2,1)S(1)}, u32[]{:S(2)}, u32[]{:S(2)}) %collective-permute-start.5) | collective-permute-done | bytes 131104 | tf_op jit(solution)/shard_map/ppermute | solution.py:19
  47.0 4.6 %collective-permute-start.6 = (bf16[1,64,4,1,128]{4,1,3,2,0:T(8,128)(2,1)S(1)}, bf16[1,64,4,1,128]{4,1,3,2,0:T(8,128)(2,1)S(1)}, u32[]{:S(2)}, u32[]{:S(2)}) collective-permute-start(bf16[1,64,4,1,128]{4,1,3,2,0:T(8,128)(2,1)S(1)} %get-tuple-element.17), channel_id=1, source_target_pairs={{0,1},{1,2},{2,3},{4,5},{5,6},{6,7},{8,9},{9,10},{10,11},{12,13},{... | collective-permute-start | bytes 196616 | tf_op jit(solution)/shard_map/ppermute | solution.py:18
  51.6 1.3 collective-permute-start.7
  53.5 4.0 collective-permute-start.10
  57.5 1.5 collective-permute-start.11
  60.0 0.9 fusion.85
  61.7 1.5 convolution_bitcast_fusion
  63.3 1.3 convolution_bitcast_fusion.7
  64.7 0.9 fusion.84
  65.6 1.0 fusion.83
  68.4 0.9 fusion.80
  69.3 0.9 fusion.79
  70.3 1.3 convolution_bitcast_fusion.1
  72.5 1.0 fusion.77
  74.4 0.9 fusion.75
  75.3 0.9 fusion.74
  76.2 0.9 fusion.73
  77.2 0.9 fusion.72
  78.1 0.9 fusion.71
  79.0 0.9 fusion.70
  80.8 0.9 fusion.68
  81.8 0.9 fusion.67
  83.6 0.9 fusion.65
  85.5 0.9 fusion.63
  86.4 1.0 fusion.62
  87.3 0.9 fusion.61
  88.3 0.9 fusion.60
  89.2 0.9 fusion.59
  92.3 1.5 convolution_add_fusion.7
  93.8 1.3 convolution_bitcast_fusion.2
  95.1 1.4 convolution_bitcast_fusion.3
  96.6 1.7 fusion.5
  111.9 1.8 copy.63
  113.8 2.1 convolution_bitcast_fusion.5
  115.9 4.0 copy.91
  120.0 2.3 convolution_bitcast_fusion.6
  122.3 2.1 convolution_add_fusion.6
  124.7 2.1 convolution_bitcast_fusion.8
  126.8 2.2 convolution_bitcast_fusion.9
  129.0 1.3 convolution_add_fusion.5
  130.3 1.2 convolution_add_fusion.4
  131.5 1.1 convolution_add_fusion.3
  132.6 1.1 convolution_add_fusion.2
  133.7 1.2 convolution_add_fusion.1
  134.9 1.1 fusion.7
  135.9 53.8 %reduce-scatter.3.cloned.1.call-done = f32[27,4,32]{2,0,1:T(8,128)} async-done(((f32[27,64,32]{2,0,1:T(8,128)}), f32[27,4,32]{2,0,1:T(8,128)}) %reduce-scatter.3.cloned.1.call-update) | async-done | bytes 13840 | tf_op jit(solution)/shard_map/reduce_scatter | solution.py:83
  189.8 76.9 %reduce-scatter.5.cloned.1.call-done = f32[27,8,64]{2,0,1:T(8,128)} async-done(((f32[27,128,64]{2,0,1:T(8,128)}), f32[27,8,64]{2,0,1:T(8,128)}) %reduce-scatter.5.cloned.1.call-update) | async-done | bytes 55312 | tf_op jit(solution)/shard_map/reduce_scatter | solution.py:84
  266.7 4.5 %fusion.27 = bf16[1,128,2,8,128]{1,4,3,2,0:T(8,128)(2,1)S(1)} fusion(f32[1,128,2,8,128]{1,4,3,2,0:T(8,128)} %convolution_bitcast_fusion, f32[1,128,2,8,128]{1,4,3,2,0:T(8,128)} %convolution_bitcast_fusion.1, f32[1,128,2,8,128]{1,4,3,2,0:T(8,128)} %convolution_bitcast_fusion.2, f32[1,128,2,8,128]{1,4,3,2,0:T(8,128)} %convolution_bitcast_fusion.3, ...), kind=kOutput, calls=%fused_computation.64 | convolution fusion | flops 36700160 | bytes 12337152 | tf_op jit(solution)/shard_map/oi,bidhw->bodhw/dot_general | solution.py:43
  271.2 1.2 copy.92
  272.4 136.0 %all-reduce.6.cloned.1.call-done = (f32[27,4,32]{2,0,1:T(8,128)}, f32[27,8,64]{2,0,1:T(8,128)}) async-done(((f32[27,4,32]{2,0,1:T(8,128)}, f32[27,8,64]{2,0,1:T(8,128)}), (f32[27,4,32]{2,0,1:T(8,128)}, f32[27,8,64]{2,0,1:T(8,128)})) %all-reduce.6.cloned.1.call-update) | async-done | bytes 69136 | tf_op jit(solution)/shard_map/psum | solution.py:81
  408.4 1.6 copy.94
  410.0 1.5 copy.93
  (143 shorter events, 33.7 us)
Async XLA Ops:
  7.2 182.6 %reduce-scatter.3.cloned.1.call-start = ((), (), s32[]{:S(2)}) async-start(), calls=%async_computation.2 | async-start | bytes 1114112 | tf_op jit(solution)/shard_map/reduce_scatter | solution.py:83
  8.2 12.1 %copy-start.5 = (bf16[1,32,2,8,128]{4,3,2,1,0:T(8,128)(2,1)S(1)}, bf16[1,32,2,8,128]{4,3,2,1,0:T(8,128)(2,1)}, u32[]{:S(2)}) copy-start(bf16[1,32,2,8,128]{4,3,2,1,0:T(8,128)(2,1)} %param.4) | copy-start | bytes 393220
  8.2 12.1 %collective-permute-start = (bf16[1,32,1,8,128]{4,1,3,2,0:T(8,128)(2,1)S(1)}, bf16[1,32,1,8,128]{4,1,3,2,0:T(8,128)(2,1)S(1)}, u32[]{:S(2)}, u32[]{:S(2)}) collective-permute-start(bf16[1,32,1,8,128]{4,1,3,2,0:T(8,128)(2,1)S(1)} %get-tuple-element.24), channel_id=1, source_target_pairs={{0,4},{4,8},{8,12},{1,5},{5,9},{9,13},{2,6},{6,10},{10,14},{3,7},{... | collective-permute-start | bytes 196616 | tf_op jit(solution)/shard_map/ppermute | solution.py:18
  11.7 11.3 %copy-start.7 = (bf16[27,64,32]{1,2,0:T(8,128)(2,1)S(1)}, bf16[27,64,32]{1,2,0:T(8,128)(2,1)}, u32[]{:S(2)}) copy-start(bf16[27,64,32]{1,2,0:T(8,128)(2,1)} %param.5) | copy-start | bytes 331780
  11.7 8.6 %collective-permute-start.1 = (bf16[1,32,1,8,128]{4,1,3,2,0:T(8,128)(2,1)S(1)}, bf16[1,32,1,8,128]{4,1,3,2,0:T(8,128)(2,1)S(1)}, u32[]{:S(2)}, u32[]{:S(2)}) collective-permute-start(bf16[1,32,1,8,128]{4,1,3,2,0:T(8,128)(2,1)S(1)} %get-tuple-element.23), channel_id=1, source_target_pairs={{4,0},{8,4},{12,8},{5,1},{9,5},{13,9},{6,2},{10,6},{14,10},{7,3},{... | collective-permute-start | bytes 196616 | tf_op jit(solution)/shard_map/ppermute | solution.py:19
  14.4 38.8 %collective-permute-start.8 = (bf16[1,128,1,8,128]{4,1,3,2,0:T(8,128)(2,1)S(1)}, bf16[1,128,1,8,128]{4,1,3,2,0:T(8,128)(2,1)S(1)}, u32[]{:S(2)}, u32[]{:S(2)}) collective-permute-start(bf16[1,128,1,8,128]{4,1,3,2,0:T(8,128)(2,1)S(1)} %get-tuple-element.14), channel_id=1, source_target_pairs={{0,4},{4,8},{8,12},{1,5},{5,9},{9,13},{2,6},{6,10},{10,14},{3,7},{... | collective-permute-start | bytes 786440 | tf_op jit(solution)/shard_map/ppermute | solution.py:18
  19.0 34.5 %collective-permute-start.9 = (bf16[1,128,1,8,128]{4,1,3,2,0:T(8,128)(2,1)S(1)}, bf16[1,128,1,8,128]{4,1,3,2,0:T(8,128)(2,1)S(1)}, u32[]{:S(2)}, u32[]{:S(2)}) collective-permute-start(bf16[1,128,1,8,128]{4,1,3,2,0:T(8,128)(2,1)S(1)} %get-tuple-element.13), channel_id=1, source_target_pairs={{4,0},{8,4},{12,8},{5,1},{9,5},{13,9},{6,2},{10,6},{14,10},{7,3},{... | collective-permute-start | bytes 786440 | tf_op jit(solution)/shard_map/ppermute | solution.py:19
  20.4 2.9 collective-permute-start.2
  21.7 5.6 %collective-permute-start.3 = (bf16[1,32,4,1,128]{4,1,3,2,0:T(8,128)(2,1)S(1)}, bf16[1,32,4,1,128]{4,1,3,2,0:T(8,128)(2,1)S(1)}, u32[]{:S(2)}, u32[]{:S(2)}) collective-permute-start(bf16[1,32,4,1,128]{4,1,3,2,0:T(8,128)(2,1)S(1)} %get-tuple-element.22), channel_id=1, source_target_pairs={{1,0},{2,1},{3,2},{5,4},{6,5},{7,6},{9,8},{10,9},{11,10},{13,12},{... | collective-permute-start | bytes 98312 | tf_op jit(solution)/shard_map/ppermute | solution.py:19
  34.9 6.5 %copy-start = (bf16[1,128,2,8,128]{4,3,2,1,0:T(8,128)(2,1)S(1)}, bf16[1,128,2,8,128]{4,3,2,1,0:T(8,128)(2,1)}, u32[]{:S(2)}) copy-start(bf16[1,128,2,8,128]{4,3,2,1,0:T(8,128)(2,1)} %param.7) | copy-start | bytes 1572868
  34.9 6.5 %copy-start.6 = (bf16[27,128,64]{1,2,0:T(8,128)(2,1)S(1)}, bf16[27,128,64]{1,2,0:T(8,128)(2,1)}, u32[]{:S(2)}) copy-start(bf16[27,128,64]{1,2,0:T(8,128)(2,1)} %param.6) | copy-start | bytes 1327108
  35.5 7.1 %collective-permute-start.4 = (bf16[1,64,1,8,128]{4,1,3,2,0:T(8,128)(2,1)S(1)}, bf16[1,64,1,8,128]{4,1,3,2,0:T(8,128)(2,1)S(1)}, u32[]{:S(2)}, u32[]{:S(2)}) collective-permute-start(bf16[1,64,1,8,128]{4,1,3,2,0:T(8,128)(2,1)S(1)} %get-tuple-element.19), channel_id=1, source_target_pairs={{0,4},{4,8},{8,12},{1,5},{5,9},{9,13},{2,6},{6,10},{10,14},{3,7},{... | collective-permute-start | bytes 393224 | tf_op jit(solution)/shard_map/ppermute | solution.py:18
  40.1 6.9 %collective-permute-start.5 = (bf16[1,64,1,8,128]{4,1,3,2,0:T(8,128)(2,1)S(1)}, bf16[1,64,1,8,128]{4,1,3,2,0:T(8,128)(2,1)S(1)}, u32[]{:S(2)}, u32[]{:S(2)}) collective-permute-start(bf16[1,64,1,8,128]{4,1,3,2,0:T(8,128)(2,1)S(1)} %get-tuple-element.20), channel_id=1, source_target_pairs={{4,0},{8,4},{12,8},{5,1},{9,5},{13,9},{6,2},{10,6},{14,10},{7,3},{... | collective-permute-start | bytes 393224 | tf_op jit(solution)/shard_map/ppermute | solution.py:19
  47.0 12.2 %collective-permute-start.6 = (bf16[1,64,4,1,128]{4,1,3,2,0:T(8,128)(2,1)S(1)}, bf16[1,64,4,1,128]{4,1,3,2,0:T(8,128)(2,1)S(1)}, u32[]{:S(2)}, u32[]{:S(2)}) collective-permute-start(bf16[1,64,4,1,128]{4,1,3,2,0:T(8,128)(2,1)S(1)} %get-tuple-element.17), channel_id=1, source_target_pairs={{0,1},{1,2},{2,3},{4,5},{5,6},{6,7},{8,9},{9,10},{10,11},{12,13},{... | collective-permute-start | bytes 196616 | tf_op jit(solution)/shard_map/ppermute | solution.py:18
  51.6 7.6 %collective-permute-start.7 = (bf16[1,64,4,1,128]{4,1,3,2,0:T(8,128)(2,1)S(1)}, bf16[1,64,4,1,128]{4,1,3,2,0:T(8,128)(2,1)S(1)}, u32[]{:S(2)}, u32[]{:S(2)}) collective-permute-start(bf16[1,64,4,1,128]{4,1,3,2,0:T(8,128)(2,1)S(1)} %get-tuple-element.18), channel_id=1, source_target_pairs={{1,0},{2,1},{3,2},{5,4},{6,5},{7,6},{9,8},{10,9},{11,10},{13,12},{... | collective-permute-start | bytes 196616 | tf_op jit(solution)/shard_map/ppermute | solution.py:19
  53.5 43.1 %collective-permute-start.10 = (bf16[1,128,4,1,128]{4,1,3,2,0:T(8,128)(2,1)S(1)}, bf16[1,128,4,1,128]{4,1,3,2,0:T(8,128)(2,1)S(1)}, u32[]{:S(2)}, u32[]{:S(2)}) collective-permute-start(bf16[1,128,4,1,128]{4,1,3,2,0:T(8,128)(2,1)S(1)} %get-tuple-element.11), channel_id=1, source_target_pairs={{0,1},{1,2},{2,3},{4,5},{5,6},{6,7},{8,9},{9,10},{10,11},{12,13},{... | collective-permute-start | bytes 393224 | tf_op jit(solution)/shard_map/ppermute | solution.py:18
  57.5 39.1 %collective-permute-start.11 = (bf16[1,128,4,1,128]{4,1,3,2,0:T(8,128)(2,1)S(1)}, bf16[1,128,4,1,128]{4,1,3,2,0:T(8,128)(2,1)S(1)}, u32[]{:S(2)}, u32[]{:S(2)}) collective-permute-start(bf16[1,128,4,1,128]{4,1,3,2,0:T(8,128)(2,1)S(1)} %get-tuple-element.12), channel_id=1, source_target_pairs={{1,0},{2,1},{3,2},{5,4},{6,5},{7,6},{9,8},{10,9},{11,10},{13,12},{... | collective-permute-start | bytes 393224 | tf_op jit(solution)/shard_map/ppermute | solution.py:19
  63.3 26.8 %copy-start.4 = (bf16[1,64,4,9,128]{4,1,3,2,0:T(8,128)(2,1)}, bf16[1,64,4,9,128]{4,1,3,2,0:T(8,128)(2,1)S(1)}, u32[]{:S(2)}) copy-start(bf16[1,64,4,9,128]{4,1,3,2,0:T(8,128)(2,1)S(1)} %get-tuple-element.15) | copy-start | bytes 1769476
  63.3 28.7 %copy-start.3 = (bf16[1,64,4,9,128]{4,1,3,2,0:T(8,128)(2,1)}, bf16[1,64,4,9,128]{4,1,3,2,0:T(8,128)(2,1)S(1)}, u32[]{:S(2)}) copy-start(bf16[1,64,4,9,128]{4,1,3,2,0:T(8,128)(2,1)S(1)} %get-tuple-element.16) | copy-start | bytes 1769476
  113.8 152.9 %reduce-scatter.5.cloned.1.call-start = ((), (), s32[]{:S(2)}) async-start(), calls=%async_computation.3 | async-start | bytes 2228224 | tf_op jit(solution)/shard_map/reduce_scatter | solution.py:84
  120.0 2.3 copy-start.1
  124.4 284.0 %all-reduce.6.cloned.1.call-start = ((), (), s32[]{:S(2)}) async-start(), calls=%async_computation.4 | async-start | bytes 393216 | tf_op jit(solution)/shard_map/psum | solution.py:81
  124.7 4.3 %copy-start.2 = (f32[2,8,128,128]{3,2,1,0:T(8,128)S(1)}, f32[2,8,128,128]{3,2,1,0:T(8,128)}, u32[]{:S(2)}) copy-start(f32[2,8,128,128]{3,2,1,0:T(8,128)} %convolution_add_fusion.6) | copy-start | bytes 3145732
Sparse Core Ops, SparseCore 0:
  113.9 75.8 reduce-scatter.2
  192.5 74.1 reduce-scatter.4
  269.6 138.7 all-reduce.5
where the time goes:
time: 419 us; the launch traced here: 418 us
  waiting for transfers between devices  276 us (66%)
  matrix products  80.8 us (19%)
  starting transfers between devices  31 us (7%)
  between operations  14.5 us (3%)
  local copies, waits for them, and re-layouts  12.7 us (3%)
    psum x1, waiting for transfers between devices, per_device(): summed = lax.psum((grad_first, grad_second), ('dep', 'hgt'))  136 us
    reduce_scatter x1, waiting for transfers between devices, per_device(): lax.psum_scatter(summed[1], 'dp', scatter_dimension=1, tiled=True)  76.9 us
    reduce_scatter x1, waiting for transfers between devices, per_device(): lax.psum_scatter(summed[0], 'dp', scatter_dimension=1, tiled=True)  53.8 us
    dot_general x54, matrix products, convolve(): jnp.einsum('oi,bidhw->bodhw', kernel[number], piece, preferred_element_ty...  41.9 us
    dot_general x54, matrix products, kernel_grad(): jnp.einsum('bodhw,bidhw->oi', upstream, piece, preferred_element_type=jnp...  31.1 us
    ppermute x6, starting transfers between devices, extended_2(): before = lax.ppermute(last, axis, up)  22.5 us
    ppermute x6, waiting for transfers between devices, extended_2(): after = lax.ppermute(leading, axis, down)  8.42 us
  transfers between devices with their start and end apart: 15, of which 6 were waited for; matrix products, arithmetic and copies ran while one was open for 18% of the time, Pallas kernels for 0%

commit v1 on v0

--- a/solution.py
+++ b/solution.py
@@ -78,7 +78,7 @@
     sigma = jax.nn.sigmoid(pre)
     delta = (back * (sigma * (1.0 + pre * (1.0 - sigma)))).astype(jnp.bfloat16)
     grad_first = kernel_grad(delta, vol_rim, depth, height, width)
-    summed = lax.psum((grad_first, grad_second), ("dep", "hgt"))
+    summed = jax.lax.psum(jax.lax.psum((grad_first, grad_second), "hgt"), "dep")
     grad_first, grad_second = (
         lax.psum_scatter(summed[0], "dp", scatter_dimension=1, tiled=True),
         lax.psum_scatter(summed[1], "dp", scatter_dimension=1, tiled=True),

time: 419 us -> 374 us (0.89)
  waiting for transfers between devices: 276 us -> 230 us
    psum x1 -> x2, waiting for transfers between devices: 136 us -> 90.1 us  [per_device(): summed = jax.lax.psum(jax.lax.psum((grad_first, grad_second), 'hgt'), 'dep')]
  transfers between devices with their start and end apart: 15 -> 16, of which waited for: 6 -> 7; matrix products, arithmetic and copies ran while one was open for 18% -> 20% of each run, Pallas kernels for 0% -> 0%
where the time goes in v1:
time: 374 us; the launch traced here: 373 us
  waiting for transfers between devices  230 us (61%)
  matrix products  81.6 us (22%)
  starting transfers between devices  31 us (8%)
  between operations  14.5 us (4%)
  local copies, waits for them, and re-layouts  12.7 us (3%)
    psum x2, waiting for transfers between devices, per_device(): summed = jax.lax.psum(jax.lax.psum((grad_first, grad_second), 'hgt'), 'dep')  90.1 us
    reduce_scatter x1, waiting for transfers between devices, per_device(): lax.psum_scatter(summed[1], 'dp', scatter_dimension=1, tiled=True)  76.8 us
    reduce_scatter x1, waiting for transfers between devices, per_device(): lax.psum_scatter(summed[0], 'dp', scatter_dimension=1, tiled=True)  53.9 us
    dot_general x54, matrix products, convolve(): jnp.einsum('oi,bidhw->bodhw', kernel[number], piece, preferred_element_ty...  42.6 us
    dot_general x54, matrix products, kernel_grad(): jnp.einsum('bodhw,bidhw->oi', upstream, piece, preferred_element_type=jnp...  31.1 us
    ppermute x6, starting transfers between devices, extended_2(): before = lax.ppermute(last, axis, up)  22.5 us
    ppermute x6, waiting for transfers between devices, extended_2(): after = lax.ppermute(leading, axis, down)  8.42 us
    ppermute x6, starting transfers between devices, extended_2(): after = lax.ppermute(leading, axis, down)  8.06 us
  transfers between devices with their start and end apart: 16, of which 7 were waited for; matrix products, arithmetic and copies ran while one was open for 20% of the time, Pallas kernels for 0%

profile of v1, /device:TPU:8, one launch (start us, length us, event | category | flops | bytes accessed | tf_op | source)
XLA Modules:
  0.0 373.0 jit_solution(4920711104044550527)
XLA Ops:
  7.2 0.9 copy.50
  8.2 3.5 collective-permute-start
  11.7 1.4 collective-permute-start.1
  13.2 1.2 copy.56
  14.4 4.6 %collective-permute-start.8 = (bf16[1,128,1,8,128]{4,1,3,2,0:T(8,128)(2,1)S(1)}, bf16[1,128,1,8,128]{4,1,3,2,0:T(8,128)(2,1)S(1)}, u32[]{:S(2)}, u32[]{:S(2)}) collective-permute-start(bf16[1,128,1,8,128]{4,1,3,2,0:T(8,128)(2,1)S(1)} %get-tuple-element.16), channel_id=1, source_target_pairs={{0,4},{4,8},{8,12},{1,5},{5,9},{9,13},{2,6},{6,10},{10,14},{3,7},{... | collective-permute-start | bytes 786440 | tf_op jit(solution)/shard_map/ppermute | solution.py:18
  19.0 1.3 collective-permute-start.9
  20.4 1.3 collective-permute-start.2
  21.7 1.3 collective-permute-start.3
  23.3 4.0 %collective-permute-done.3 = bf16[1,32,4,1,128]{4,1,3,2,0:T(8,128)(2,1)S(1)} collective-permute-done((bf16[1,32,4,1,128]{4,1,3,2,0:T(8,128)(2,1)S(1)}, bf16[1,32,4,1,128]{4,1,3,2,0:T(8,128)(2,1)S(1)}, u32[]{:S(2)}, u32[]{:S(2)}) %collective-permute-start.3) | collective-permute-done | bytes 32800 | tf_op jit(solution)/shard_map/ppermute | solution.py:19
  35.5 4.6 %collective-permute-start.4 = (bf16[1,64,1,8,128]{4,1,3,2,0:T(8,128)(2,1)S(1)}, bf16[1,64,1,8,128]{4,1,3,2,0:T(8,128)(2,1)S(1)}, u32[]{:S(2)}, u32[]{:S(2)}) collective-permute-start(bf16[1,64,1,8,128]{4,1,3,2,0:T(8,128)(2,1)S(1)} %get-tuple-element.21), channel_id=1, source_target_pairs={{0,4},{4,8},{8,12},{1,5},{5,9},{9,13},{2,6},{6,10},{10,14},{3,7},{... | collective-permute-start | bytes 393224 | tf_op jit(solution)/shard_map/ppermute | solution.py:18
  40.1 1.3 collective-permute-start.5
  41.6 0.9 collective-permute-done.4
  42.6 4.4 %collective-permute-done.5 = bf16[1,64,1,8,128]{4,1,3,2,0:T(8,128)(2,1)S(1)} collective-permute-done((bf16[1,64,1,8,128]{4,1,3,2,0:T(8,128)(2,1)S(1)}, bf16[1,64,1,8,128]{4,1,3,2,0:T(8,128)(2,1)S(1)}, u32[]{:S(2)}, u32[]{:S(2)}) %collective-permute-start.5) | collective-permute-done | bytes 131104 | tf_op jit(solution)/shard_map/ppermute | solution.py:19
  47.0 4.6 %collective-permute-start.6 = (bf16[1,64,4,1,128]{4,1,3,2,0:T(8,128)(2,1)S(1)}, bf16[1,64,4,1,128]{4,1,3,2,0:T(8,128)(2,1)S(1)}, u32[]{:S(2)}, u32[]{:S(2)}) collective-permute-start(bf16[1,64,4,1,128]{4,1,3,2,0:T(8,128)(2,1)S(1)} %get-tuple-element.19), channel_id=1, source_target_pairs={{0,1},{1,2},{2,3},{4,5},{5,6},{6,7},{8,9},{9,10},{10,11},{12,13},{... | collective-permute-start | bytes 196616 | tf_op jit(solution)/shard_map/ppermute | solution.py:18
  51.6 1.3 collective-permute-start.7
  53.5 4.0 %collective-permute-start.10 = (bf16[1,128,4,1,128]{4,1,3,2,0:T(8,128)(2,1)S(1)}, bf16[1,128,4,1,128]{4,1,3,2,0:T(8,128)(2,1)S(1)}, u32[]{:S(2)}, u32[]{:S(2)}) collective-permute-start(bf16[1,128,4,1,128]{4,1,3,2,0:T(8,128)(2,1)S(1)} %get-tuple-element.13), channel_id=1, source_target_pairs={{0,1},{1,2},{2,3},{4,5},{5,6},{6,7},{8,9},{9,10},{10,11},{12,13},{... | collective-permute-start | bytes 393224 | tf_op jit(solution)/shard_map/ppermute | solution.py:18
  57.5 1.5 collective-permute-start.11
  60.0 0.9 fusion.85
  61.9 1.3 convolution_bitcast_fusion.7
  64.1 0.9 fusion.83
  66.0 0.9 fusion.81
  66.9 1.0 fusion.80
  68.8 1.3 convolution_bitcast_fusion.1
  70.1 0.9 fusion.78
  71.0 1.0 fusion.77
  73.8 1.0 fusion.74
  74.7 0.9 fusion.73
  75.7 0.9 fusion.72
  76.6 1.0 fusion.71
  77.5 0.9 fusion.70
  78.5 0.9 fusion.69
  79.4 1.0 fusion.68
  81.2 0.9 fusion.66
  82.2 0.9 fusion.65
  83.1 0.9 fusion.64
  84.9 1.0 fusion.62
  85.9 0.9 fusion.61
  87.7 0.9 fusion.59
  90.9 1.5 convolution_add_fusion.7
  92.4 1.5 convolution_bitcast_fusion
  93.9 1.3 convolution_bitcast_fusion.2
  95.2 1.7 fusion.5
  110.6 1.8 copy.63
  112.5 2.2 convolution_bitcast_fusion.3
  114.6 4.0 %copy.91 = f32[27,128,64]{2,0,1:T(8,128)} copy(f32[27,128,64]{1,2,0:T(8,128)} %fusion.59) | data formatting | bytes 1769472 | tf_op jit(solution)/shard_map/stack | solution.py:58
  118.6 2.2 convolution_bitcast_fusion.5
  120.8 2.1 convolution_add_fusion.6
  123.3 2.3 convolution_bitcast_fusion.6
  125.6 2.0 convolution_bitcast_fusion.8
  127.6 1.3 convolution_add_fusion.5
  128.9 1.2 convolution_add_fusion.4
  130.1 1.1 convolution_add_fusion.3
  131.2 1.1 convolution_add_fusion.2
  132.3 1.2 convolution_add_fusion.1
  133.5 1.1 fusion.7
  134.5 53.9 %reduce-scatter.3.cloned.1.call-done = f32[27,4,32]{2,0,1:T(8,128)} async-done(((f32[27,64,32]{2,0,1:T(8,128)}), f32[27,4,32]{2,0,1:T(8,128)}) %reduce-scatter.3.cloned.1.call-update) | async-done | bytes 13840 | tf_op jit(solution)/shard_map/reduce_scatter | solution.py:83
  188.4 76.8 %reduce-scatter.5.cloned.1.call-done = f32[27,8,64]{2,0,1:T(8,128)} async-done(((f32[27,128,64]{2,0,1:T(8,128)}), f32[27,8,64]{2,0,1:T(8,128)}) %reduce-scatter.5.cloned.1.call-update) | async-done | bytes 55312 | tf_op jit(solution)/shard_map/reduce_scatter | solution.py:84
  265.3 2.2 convolution_bitcast_fusion.9
  267.5 46.6 %all-reduce.8.cloned.1.call-done = (f32[27,4,32]{2,0,1:T(8,128)}, f32[27,8,64]{2,0,1:T(8,128)}) async-done(((f32[27,4,32]{2,0,1:T(8,128)}, f32[27,8,64]{2,0,1:T(8,128)}), (f32[27,4,32]{2,0,1:T(8,128)}, f32[27,8,64]{2,0,1:T(8,128)})) %all-reduce.8.cloned.1.call-update) | async-done | bytes 69136 | tf_op jit(solution)/shard_map/psum | solution.py:81
  314.2 4.5 %fusion.27 = bf16[1,128,2,8,128]{1,4,3,2,0:T(8,128)(2,1)S(1)} fusion(f32[1,128,2,8,128]{1,4,3,2,0:T(8,128)} %convolution_bitcast_fusion, f32[1,128,2,8,128]{1,4,3,2,0:T(8,128)} %convolution_bitcast_fusion.1, f32[1,128,2,8,128]{1,4,3,2,0:T(8,128)} %convolution_bitcast_fusion.2, f32[1,128,2,8,128]{1,4,3,2,0:T(8,128)} %convolution_bitcast_fusion.3, ...), kind=kOutput, calls=%fused_computation.64 | convolution fusion | flops 36700160 | bytes 12337152 | tf_op jit(solution)/shard_map/oi,bidhw->bodhw/dot_general | solution.py:43
  318.7 1.2 copy.92
  319.9 43.4 %all-reduce.10.cloned.1.call-done = (f32[27,4,32]{2,0,1:T(8,128)}, f32[27,8,64]{2,0,1:T(8,128)}) async-done(((f32[27,4,32]{2,0,1:T(8,128)}, f32[27,8,64]{2,0,1:T(8,128)}), (f32[27,4,32]{2,0,1:T(8,128)}, f32[27,8,64]{2,0,1:T(8,128)})) %all-reduce.10.cloned.1.call-update) | async-done | bytes 69136 | tf_op jit(solution)/shard_map/psum | solution.py:81
  363.3 1.6 copy.94
  364.9 1.5 copy.93
  (146 shorter events, 34.7 us)
Async XLA Ops:
  7.2 181.3 %reduce-scatter.3.cloned.1.call-start = ((), (), s32[]{:S(2)}) async-start(), calls=%async_computation.2 | async-start | bytes 1114112 | tf_op jit(solution)/shard_map/reduce_scatter | solution.py:83
  8.2 12.1 %copy-start.5 = (bf16[1,32,2,8,128]{4,3,2,1,0:T(8,128)(2,1)S(1)}, bf16[1,32,2,8,128]{4,3,2,1,0:T(8,128)(2,1)}, u32[]{:S(2)}) copy-start(bf16[1,32,2,8,128]{4,3,2,1,0:T(8,128)(2,1)} %param.4) | copy-start | bytes 393220
  8.2 12.1 %collective-permute-start = (bf16[1,32,1,8,128]{4,1,3,2,0:T(8,128)(2,1)S(1)}, bf16[1,32,1,8,128]{4,1,3,2,0:T(8,128)(2,1)S(1)}, u32[]{:S(2)}, u32[]{:S(2)}) collective-permute-start(bf16[1,32,1,8,128]{4,1,3,2,0:T(8,128)(2,1)S(1)} %get-tuple-element.26), channel_id=1, source_target_pairs={{0,4},{4,8},{8,12},{1,5},{5,9},{9,13},{2,6},{6,10},{10,14},{3,7},{... | collective-permute-start | bytes 196616 | tf_op jit(solution)/shard_map/ppermute | solution.py:18
  11.7 11.3 %copy-start.7 = (bf16[27,64,32]{1,2,0:T(8,128)(2,1)S(1)}, bf16[27,64,32]{1,2,0:T(8,128)(2,1)}, u32[]{:S(2)}) copy-start(bf16[27,64,32]{1,2,0:T(8,128)(2,1)} %param.5) | copy-start | bytes 331780
  11.7 8.6 %collective-permute-start.1 = (bf16[1,32,1,8,128]{4,1,3,2,0:T(8,128)(2,1)S(1)}, bf16[1,32,1,8,128]{4,1,3,2,0:T(8,128)(2,1)S(1)}, u32[]{:S(2)}, u32[]{:S(2)}) collective-permute-start(bf16[1,32,1,8,128]{4,1,3,2,0:T(8,128)(2,1)S(1)} %get-tuple-element.25), channel_id=1, source_target_pairs={{4,0},{8,4},{12,8},{5,1},{9,5},{13,9},{6,2},{10,6},{14,10},{7,3},{... | collective-permute-start | bytes 196616 | tf_op jit(solution)/shard_map/ppermute | solution.py:19
  14.4 38.8 %collective-permute-start.8 = (bf16[1,128,1,8,128]{4,1,3,2,0:T(8,128)(2,1)S(1)}, bf16[1,128,1,8,128]{4,1,3,2,0:T(8,128)(2,1)S(1)}, u32[]{:S(2)}, u32[]{:S(2)}) collective-permute-start(bf16[1,128,1,8,128]{4,1,3,2,0:T(8,128)(2,1)S(1)} %get-tuple-element.16), channel_id=1, source_target_pairs={{0,4},{4,8},{8,12},{1,5},{5,9},{9,13},{2,6},{6,10},{10,14},{3,7},{... | collective-permute-start | bytes 786440 | tf_op jit(solution)/shard_map/ppermute | solution.py:18
  19.0 34.5 %collective-permute-start.9 = (bf16[1,128,1,8,128]{4,1,3,2,0:T(8,128)(2,1)S(1)}, bf16[1,128,1,8,128]{4,1,3,2,0:T(8,128)(2,1)S(1)}, u32[]{:S(2)}, u32[]{:S(2)}) collective-permute-start(bf16[1,128,1,8,128]{4,1,3,2,0:T(8,128)(2,1)S(1)} %get-tuple-element.15), channel_id=1, source_target_pairs={{4,0},{8,4},{12,8},{5,1},{9,5},{13,9},{6,2},{10,6},{14,10},{7,3},{... | collective-permute-start | bytes 786440 | tf_op jit(solution)/shard_map/ppermute | solution.py:19
  20.4 2.9 collective-permute-start.2
  21.7 5.6 %collective-permute-start.3 = (bf16[1,32,4,1,128]{4,1,3,2,0:T(8,128)(2,1)S(1)}, bf16[1,32,4,1,128]{4,1,3,2,0:T(8,128)(2,1)S(1)}, u32[]{:S(2)}, u32[]{:S(2)}) collective-permute-start(bf16[1,32,4,1,128]{4,1,3,2,0:T(8,128)(2,1)S(1)} %get-tuple-element.24), channel_id=1, source_target_pairs={{1,0},{2,1},{3,2},{5,4},{6,5},{7,6},{9,8},{10,9},{11,10},{13,12},{... | collective-permute-start | bytes 98312 | tf_op jit(solution)/shard_map/ppermute | solution.py:19
  34.9 6.5 %copy-start = (bf16[1,128,2,8,128]{4,3,2,1,0:T(8,128)(2,1)S(1)}, bf16[1,128,2,8,128]{4,3,2,1,0:T(8,128)(2,1)}, u32[]{:S(2)}) copy-start(bf16[1,128,2,8,128]{4,3,2,1,0:T(8,128)(2,1)} %param.7) | copy-start | bytes 1572868
  34.9 6.5 %copy-start.6 = (bf16[27,128,64]{1,2,0:T(8,128)(2,1)S(1)}, bf16[27,128,64]{1,2,0:T(8,128)(2,1)}, u32[]{:S(2)}) copy-start(bf16[27,128,64]{1,2,0:T(8,128)(2,1)} %param.6) | copy-start | bytes 1327108
  35.5 7.1 %collective-permute-start.4 = (bf16[1,64,1,8,128]{4,1,3,2,0:T(8,128)(2,1)S(1)}, bf16[1,64,1,8,128]{4,1,3,2,0:T(8,128)(2,1)S(1)}, u32[]{:S(2)}, u32[]{:S(2)}) collective-permute-start(bf16[1,64,1,8,128]{4,1,3,2,0:T(8,128)(2,1)S(1)} %get-tuple-element.21), channel_id=1, source_target_pairs={{0,4},{4,8},{8,12},{1,5},{5,9},{9,13},{2,6},{6,10},{10,14},{3,7},{... | collective-permute-start | bytes 393224 | tf_op jit(solution)/shard_map/ppermute | solution.py:18
  40.1 6.9 %collective-permute-start.5 = (bf16[1,64,1,8,128]{4,1,3,2,0:T(8,128)(2,1)S(1)}, bf16[1,64,1,8,128]{4,1,3,2,0:T(8,128)(2,1)S(1)}, u32[]{:S(2)}, u32[]{:S(2)}) collective-permute-start(bf16[1,64,1,8,128]{4,1,3,2,0:T(8,128)(2,1)S(1)} %get-tuple-element.22), channel_id=1, source_target_pairs={{4,0},{8,4},{12,8},{5,1},{9,5},{13,9},{6,2},{10,6},{14,10},{7,3},{... | collective-permute-start | bytes 393224 | tf_op jit(solution)/shard_map/ppermute | solution.py:19
  47.0 12.2 %collective-permute-start.6 = (bf16[1,64,4,1,128]{4,1,3,2,0:T(8,128)(2,1)S(1)}, bf16[1,64,4,1,128]{4,1,3,2,0:T(8,128)(2,1)S(1)}, u32[]{:S(2)}, u32[]{:S(2)}) collective-permute-start(bf16[1,64,4,1,128]{4,1,3,2,0:T(8,128)(2,1)S(1)} %get-tuple-element.19), channel_id=1, source_target_pairs={{0,1},{1,2},{2,3},{4,5},{5,6},{6,7},{8,9},{9,10},{10,11},{12,13},{... | collective-permute-start | bytes 196616 | tf_op jit(solution)/shard_map/ppermute | solution.py:18
  51.6 7.6 %collective-permute-start.7 = (bf16[1,64,4,1,128]{4,1,3,2,0:T(8,128)(2,1)S(1)}, bf16[1,64,4,1,128]{4,1,3,2,0:T(8,128)(2,1)S(1)}, u32[]{:S(2)}, u32[]{:S(2)}) collective-permute-start(bf16[1,64,4,1,128]{4,1,3,2,0:T(8,128)(2,1)S(1)} %get-tuple-element.20), channel_id=1, source_target_pairs={{1,0},{2,1},{3,2},{5,4},{6,5},{7,6},{9,8},{10,9},{11,10},{13,12},{... | collective-permute-start | bytes 196616 | tf_op jit(solution)/shard_map/ppermute | solution.py:19
  53.5 41.7 %collective-permute-start.10 = (bf16[1,128,4,1,128]{4,1,3,2,0:T(8,128)(2,1)S(1)}, bf16[1,128,4,1,128]{4,1,3,2,0:T(8,128)(2,1)S(1)}, u32[]{:S(2)}, u32[]{:S(2)}) collective-permute-start(bf16[1,128,4,1,128]{4,1,3,2,0:T(8,128)(2,1)S(1)} %get-tuple-element.13), channel_id=1, source_target_pairs={{0,1},{1,2},{2,3},{4,5},{5,6},{6,7},{8,9},{9,10},{10,11},{12,13},{... | collective-permute-start | bytes 393224 | tf_op jit(solution)/shard_map/ppermute | solution.py:18
  57.5 37.7 %collective-permute-start.11 = (bf16[1,128,4,1,128]{4,1,3,2,0:T(8,128)(2,1)S(1)}, bf16[1,128,4,1,128]{4,1,3,2,0:T(8,128)(2,1)S(1)}, u32[]{:S(2)}, u32[]{:S(2)}) collective-permute-start(bf16[1,128,4,1,128]{4,1,3,2,0:T(8,128)(2,1)S(1)} %get-tuple-element.14), channel_id=1, source_target_pairs={{1,0},{2,1},{3,2},{5,4},{6,5},{7,6},{9,8},{10,9},{11,10},{13,12},{... | collective-permute-start | bytes 393224 | tf_op jit(solution)/shard_map/ppermute | solution.py:19
  61.9 26.8 %copy-start.4 = (bf16[1,64,4,9,128]{4,1,3,2,0:T(8,128)(2,1)}, bf16[1,64,4,9,128]{4,1,3,2,0:T(8,128)(2,1)S(1)}, u32[]{:S(2)}) copy-start(bf16[1,64,4,9,128]{4,1,3,2,0:T(8,128)(2,1)S(1)} %get-tuple-element.17) | copy-start | bytes 1769476
  61.9 28.7 %copy-start.3 = (bf16[1,64,4,9,128]{4,1,3,2,0:T(8,128)(2,1)}, bf16[1,64,4,9,128]{4,1,3,2,0:T(8,128)(2,1)S(1)}, u32[]{:S(2)}) copy-start(bf16[1,64,4,9,128]{4,1,3,2,0:T(8,128)(2,1)S(1)} %get-tuple-element.18) | copy-start | bytes 1769476
  112.4 152.9 %reduce-scatter.5.cloned.1.call-start = ((), (), s32[]{:S(2)}) async-start(), calls=%async_computation.3 | async-start | bytes 2228224 | tf_op jit(solution)/shard_map/reduce_scatter | solution.py:84
  118.6 2.2 copy-start.1
  122.9 191.2 %all-reduce.8.cloned.1.call-start = ((), (), s32[]{:S(2)}) async-start(), calls=%async_computation.4 | async-start | bytes 393216 | tf_op jit(solution)/shard_map/psum | solution.py:81
  123.2 4.4 %copy-start.2 = (f32[2,8,128,128]{3,2,1,0:T(8,128)S(1)}, f32[2,8,128,128]{3,2,1,0:T(8,128)}, u32[]{:S(2)}) copy-start(f32[2,8,128,128]{3,2,1,0:T(8,128)} %convolution_add_fusion.6) | copy-start | bytes 3145732
  265.3 98.1 %all-reduce.10.cloned.1.call-start = ((), (), s32[]{:S(2)}) async-start(), calls=%async_computation.5 | async-start | bytes 393216 | tf_op jit(solution)/shard_map/psum | solution.py:81
Sparse Core Ops, SparseCore 0:
  112.5 75.8 reduce-scatter.2
  191.1 74.0 reduce-scatter.4
  268.1 45.9 all-reduce.7
  316.4 46.9 all-reduce.9
